TPU v7x, 32 devices: a whole 2x2x4 slice. The times are simulated.
32 devices in a mesh: batch: 4 (over y, x), rows: 8 (over z, core).
Axes of the slice: x: 2, y: 2, z: 4, core: 2. Of those that a mesh axis runs over, the one named last changes fastest.
Arguments:
- features: bfloat16 [256, 8, 16, 2048], P('batch', 'rows'), may hold values from -6 to 6
- w_reduce: bfloat16 [2048, 512], P('rows'), may hold values from -0.125 to 0.125
- w_spatial: bfloat16 [4608, 512], P('rows'), may hold values from -0.09375 to 0.09375
- w_expand: bfloat16 [512, 2048], P('rows'), may hold values from -0.25 to 0.25
- query_weight: bfloat16 [2048, 512], P('rows'), may hold values from -0.125 to 0.125
- w_key: bfloat16 [2048, 512], P('rows'), may hold values from -0.125 to 0.125
- w_value: bfloat16 [2048, 512], P('rows'), may hold values from -0.125 to 0.125
- w_out: bfloat16 [512, 2048], P('rows'), may hold values from -0.5 to 0.5
- w_head: bfloat16 [4096, 80], P('rows'), may hold values from -0.09375 to 0.09375
- gain_a: float32 [512], replicated, may hold values from 0.1 to 1.9
- bias_a: float32 [512], replicated, may hold values from -0.5 to 0.5
- gain_b: float32 [512], replicated, may hold values from 0.1 to 1.9
- bias_b: float32 [512], replicated, may hold values from -0.5 to 0.5
- gain_c: float32 [2048], replicated, may hold values from 0.1 to 1.9
- bias_c: float32 [2048], replicated, may hold values from -0.5 to 0.5
- ln_gain: float32 [512], replicated, may hold values from 0.1 to 1.9
- ln_bias: float32 [512], replicated, may hold values from -0.5 to 0.5
- head_bias: float32 [80], replicated, may hold values from -1 to 1
- bank: bfloat16 [320, 2048], P(('batch', 'rows')), may hold values from -6 to 6
- piece_box: int32 [256, 8], P(('batch', 'rows')), may hold values from 0 to 127
- piece_clip: int32 [256, 8], P(('batch', 'rows')), may hold values from 0 to 63
- send_count: int32 [256], P(('batch', 'rows')), may hold values from 0 to 8, as said below
- sample_pos: int32 [256, 224], P(('batch', 'rows')), may hold values from 0 to 15
- sample_weight: float32 [256, 224], P(('batch', 'rows')), may hold values from 0.01 to 0.06
- win_start: int32 [4096], P(('batch', 'rows')), may hold values from 0 to 60, as said below
- win_len: int32 [4096], P(('batch', 'rows')), may hold values from 20 to 40, as said below
- prob_cotangent: float32 [4096, 80], P(('batch', 'rows')), may hold values from -6 to 6
Outputs:
- probs: float32 [4096, 80], P(('batch', 'rows'))
- features_grad: bfloat16 [256, 8, 16, 2048], P('batch', 'rows')
- w_reduce_grad: float32 [2048, 512], P('rows', 'batch')
- w_spatial_grad: float32 [4608, 512], P('rows', 'batch')
- w_expand_grad: float32 [512, 2048], P('rows', 'batch')
- w_query_grad: float32 [2048, 512], P('rows', 'batch')
- w_key_grad: float32 [2048, 512], P('rows', 'batch')
- w_value_grad: float32 [2048, 512], P('rows', 'batch')
- w_out_grad: float32 [512, 2048], P('rows', 'batch')
- w_head_grad: float32 [4096, 80], P('rows', 'batch')
- gain_a_grad: float32 [512], replicated
- bias_a_grad: float32 [512], replicated
- gain_b_grad: float32 [512], replicated
- bias_b_grad: float32 [512], replicated
- gain_c_grad: float32 [2048], replicated
- bias_c_grad: float32 [2048], replicated
- ln_gain_grad: float32 [512], replicated
- ln_bias_grad: float32 [512], replicated
- classifier_bias_gradient: float32 [80], replicated
Inputs may be any that keep to these rules, and one draw needn't show every extreme that they name: `send_count`: at most 8 live slots from one device to one owner; some device sends exactly 8 to some owner in every draw. `win_len`: every window holds 20 to 40 entries, some box's exactly 40. win_start + win_len <= 80.
All inputs are finite; a program needn't handle non-finite values.
Results may differ from a plain program's by a relative error of at most 0.024.
Values may be sent and summed in bfloat16 or wider, within the bound.
A program may use at most 256 MiB of HBM per device.

v0:
```python
import jax
import jax.numpy as jnp
from jax import lax
from jax.sharding import PartitionSpec as P


def padded(cells, sides, width):
    for axis, dim in sides:
        count = lax.axis_size(axis)
        ends = count - 1
        head = lax.slice_in_dim(cells, 0, width, axis=dim)
        tail = lax.slice_in_dim(cells, cells.shape[dim] - width, cells.shape[dim], axis=dim)
        cells = jnp.concatenate(
            [
                lax.ppermute(tail, axis, [(i, (i + 1) % count) for i in range(ends)]),
                cells,
                lax.ppermute(head, axis, [((i + 1) % count, i) for i in range(ends)]),
            ],
            axis=dim,
        )
    return cells


def split_up(value, dim, peers):
    shape = value.shape
    parts = value.reshape(*shape[:dim], peers, shape[dim] // peers, *shape[dim + 1 :])
    return jnp.moveaxis(parts, dim, 0)


def sum_at_owner(value, axis, dim):
    peers = lax.axis_size(axis)
    parts = lax.all_to_all(split_up(value, dim, peers), axis, 0, 0, tiled=True)
    return jnp.sum(parts.astype(jnp.float32), axis=0)


def side_by_side(arrays, axis, dim, along):
    ends, at = ([], 0)
    for a in arrays[:-1]:
        at += a.shape[along]
        ends.append(at)
    both = jnp.concatenate(arrays, axis=along)
    return tuple(jnp.split(sum_at_owner(both, axis, dim), ends, axis=along))


def tdot(left, right):
    return lax.dot_general(
        left, right, (((0,), (0,)), ((), ())), preferred_element_type=jnp.float32
    )


def ndot(left, right):
    return lax.dot_general(
        left, right, (((1,), (1,)), ((), ())), preferred_element_type=jnp.float32
    )


def silu_slope(value):
    sig = jax.nn.sigmoid(value)
    return sig * (1.0 + value * (1.0 - sig))


def normalize(field, total_count):
    sums, squares = lax.psum((jnp.sum(field, 0), jnp.sum(field * field, 0)), ("batch", "rows"))
    centre_value = sums / total_count
    inverse = lax.rsqrt(squares / total_count - centre_value * centre_value + 1e-05)
    return ((field - centre_value) * inverse, inverse)


def segment_totals(grad, normed):
    return lax.psum((jnp.sum(grad, 0), jnp.sum(grad * normed, 0)), ("batch", "rows"))


def norm_back(grad, normed, inverse, gain, shift_sum, gain_total_grad, total_count):
    return (
        gain * inverse * (grad - shift_sum / total_count - normed * gain_total_grad / total_count)
    )


def on_device(
    features,
    w_reduce,
    w_spatial,
    w_expand,
    query_weight,
    w_key,
    w_value,
    w_out,
    w_head,
    gain_a,
    bias_a,
    gain_b,
    bias_b,
    gain_c,
    bias_c,
    ln_gain,
    ln_bias,
    head_bias,
    bank,
    piece_box,
    piece_clip,
    send_count,
    sample_pos,
    sample_weight,
    win_start,
    win_len,
    prob_cotangent,
):
    owners = lax.axis_size("rows")
    clip_dev, row_dev, col_count, d_in = features.shape
    cell_count = clip_dev * row_dev * col_count
    total_count = cell_count * owners * lax.axis_size("batch")
    w_a, w_b, w_c, w_q, w_k, w_v, w_o, w_h = (
        lax.all_gather(w_reduce, "rows", axis=0, tiled=True),
        lax.all_gather(w_spatial, "rows", axis=0, tiled=True),
        lax.all_gather(w_expand, "rows", axis=0, tiled=True),
        lax.all_gather(query_weight, "rows", axis=0, tiled=True),
        lax.all_gather(w_key, "rows", axis=0, tiled=True),
        lax.all_gather(w_value, "rows", axis=0, tiled=True),
        lax.all_gather(w_out, "rows", axis=0, tiled=True),
        lax.all_gather(w_head, "rows", axis=0, tiled=True),
    )
    d_mid = w_a.shape[1]
    flat_x = features.reshape(cell_count, d_in)
    pre_a = jnp.dot(flat_x, w_a, preferred_element_type=jnp.float32)
    hat_a, inverse_a = normalize(pre_a, total_count)
    act_a = gain_a * hat_a + bias_a
    low_a = jax.nn.silu(act_a).astype(jnp.bfloat16)
    halo_a = padded(low_a.reshape(clip_dev, row_dev, col_count, d_mid), (("rows", 1),), 1)
    halo_a = jnp.pad(halo_a, ((0, 0), (0, 0), (1, 1), (0, 0)))
    window_a = jnp.concatenate(
        [
            halo_a[:, row_step : row_step + row_dev, col_step : col_step + col_count]
            for row_step in range(3)
            for col_step in range(3)
        ],
        axis=3,
    ).reshape(cell_count, 9 * d_mid)
    pre_b = jnp.dot(window_a, w_b, preferred_element_type=jnp.float32)
    hat_b, inverse_b = normalize(pre_b, total_count)
    act_b = gain_b * hat_b + bias_b
    low_b = jax.nn.silu(act_b).astype(jnp.bfloat16)
    pre_c = jnp.dot(low_b, w_c, preferred_element_type=jnp.float32)
    hat_c, inverse_c = normalize(pre_c, total_count)
    pre_out = gain_c * hat_c + bias_c + flat_x.astype(jnp.float32)
    fmap = jax.nn.silu(pre_out).astype(jnp.bfloat16)
    capacity = piece_box.shape[1]
    samples = sample_pos.shape[1] // capacity
    slot_count = owners * capacity
    sample_cells = (
        piece_clip[:, :, None] * (row_dev * col_count)
        + sample_pos.reshape(owners, capacity, samples)
    ).reshape(slot_count, samples)
    is_live = (jnp.arange(capacity)[None, :] < send_count[:, None]).reshape(slot_count)
    slot_weights = sample_weight.reshape(slot_count, samples) * is_live[:, None].astype(jnp.float32)
    cell_ids = jnp.arange(cell_count)[None, :]
    interp_sum = jnp.zeros((slot_count, cell_count), jnp.float32)
    for sample_index in range(samples):
        interp_sum = interp_sum + jnp.where(
            sample_cells[:, sample_index, None] == cell_ids,
            slot_weights[:, sample_index, None],
            0.0,
        )
    interpolated_value = interp_sum.astype(jnp.bfloat16)
    region_parts = (
        jnp.dot(interpolated_value, fmap, preferred_element_type=jnp.float32)
        .astype(jnp.bfloat16)
        .reshape(owners, capacity, d_in)
    )
    arrived, arrived_box = (
        lax.all_to_all(region_parts, "rows", split_axis=0, concat_axis=0, tiled=True),
        lax.all_to_all(piece_box, "rows", split_axis=0, concat_axis=0, tiled=True),
    )
    box_dev = win_start.shape[0]
    flat_box = arrived_box.reshape(slot_count)
    owner_hits = (flat_box[None, :] == jnp.arange(box_dev)[:, None]).astype(jnp.bfloat16)
    pooled = jnp.dot(
        owner_hits, arrived.reshape(slot_count, d_in), preferred_element_type=jnp.float32
    )
    pooled_low = pooled.astype(jnp.bfloat16)
    keys_own = jnp.dot(bank, w_k, preferred_element_type=jnp.float32).astype(jnp.bfloat16)
    values_own = jnp.dot(bank, w_v, preferred_element_type=jnp.float32).astype(jnp.bfloat16)
    key_rows, value_rows = (
        lax.all_gather(keys_own, "rows", axis=0, tiled=True),
        lax.all_gather(values_own, "rows", axis=0, tiled=True),
    )
    bank_length = key_rows.shape[0]
    queries = jnp.dot(pooled_low, w_q, preferred_element_type=jnp.float32).astype(jnp.bfloat16)
    score_scale = d_mid ** (-0.5)
    scores = ndot(queries, key_rows) * score_scale
    positions = jnp.arange(bank_length)[None, :]
    window_mask = (positions >= win_start[:, None]) & (positions < (win_start + win_len)[:, None])
    attend = jax.nn.softmax(jnp.where(window_mask, scores, -1e30), axis=-1)
    attend_low = attend.astype(jnp.bfloat16)
    mixture = jnp.dot(attend_low, value_rows, preferred_element_type=jnp.float32)
    centred = mixture - jnp.mean(mixture, axis=-1, keepdims=True)
    inverse_z = lax.rsqrt(jnp.mean(centred * centred, axis=-1, keepdims=True) + 1e-05)
    hat_z = centred * inverse_z
    pre_ln = ln_gain * hat_z + ln_bias
    low_r = jax.nn.silu(pre_ln).astype(jnp.bfloat16)
    branch = jnp.dot(low_r, w_o, preferred_element_type=jnp.float32)
    joined = jnp.concatenate([pooled, pooled + branch], axis=1).astype(jnp.bfloat16)
    logits = jnp.dot(joined, w_h, preferred_element_type=jnp.float32) + head_bias
    likely = jax.nn.sigmoid(logits)
    d_logit = (prob_cotangent * (likely * (1.0 - likely))).astype(jnp.bfloat16)
    grad_head_bias = jnp.sum(d_logit.astype(jnp.float32), 0)
    grad_wh = tdot(joined, d_logit)
    d_joined = ndot(d_logit, w_h)
    d_pooled = d_joined[:, :d_in] + d_joined[:, d_in:]
    d_branch = d_joined[:, d_in:].astype(jnp.bfloat16)
    grad_wo = tdot(low_r, d_branch)
    d_ln = ndot(d_branch, w_o) * silu_slope(pre_ln)
    grad_ln_gain = jnp.sum(d_ln * hat_z, 0)
    grad_ln_bias = jnp.sum(d_ln, 0)
    d_hat = d_ln * ln_gain
    d_mixture = (
        inverse_z
        * (
            d_hat
            - jnp.mean(d_hat, axis=-1, keepdims=True)
            - hat_z * jnp.mean(d_hat * hat_z, axis=-1, keepdims=True)
        )
    ).astype(jnp.bfloat16)
    d_attend = ndot(d_mixture, value_rows)
    d_values = tdot(attend_low, d_mixture)
    d_scores = (attend * (d_attend - jnp.sum(d_attend * attend, axis=-1, keepdims=True))).astype(
        jnp.bfloat16
    )
    d_queries = (
        jnp.dot(d_scores, key_rows, preferred_element_type=jnp.float32) * score_scale
    ).astype(jnp.bfloat16)
    d_keys = tdot(d_scores, queries) * score_scale
    grad_wq = tdot(pooled_low, d_queries)
    d_pooled = d_pooled + ndot(d_queries, w_q)
    key_sum, value_sum = side_by_side(
        (d_keys.astype(jnp.bfloat16), d_values.astype(jnp.bfloat16)), "rows", 0, 1
    )
    grad_wk = tdot(bank, key_sum.astype(jnp.bfloat16))
    grad_wv = tdot(bank, value_sum.astype(jnp.bfloat16))
    back_pieces = jnp.take(d_pooled.astype(jnp.bfloat16), flat_box, axis=0).reshape(
        owners, capacity, d_in
    )
    returned = lax.all_to_all(back_pieces, "rows", split_axis=0, concat_axis=0, tiled=True)
    d_fmap = tdot(interpolated_value, returned.reshape(slot_count, d_in))
    d_pre = d_fmap * silu_slope(pre_out)
    head_sums = lax.psum(
        (jnp.sum(d_pre, 0), jnp.sum(d_pre * hat_c, 0), grad_ln_gain, grad_ln_bias, grad_head_bias),
        ("batch", "rows"),
    )
    d_c = norm_back(
        d_pre, hat_c, inverse_c, gain_c, head_sums[0], head_sums[1], total_count
    ).astype(jnp.bfloat16)
    grad_wc = tdot(low_b, d_c)
    d_act_b = ndot(d_c, w_c) * silu_slope(act_b)
    shift_b_sum, gain_b_sum = segment_totals(d_act_b, hat_b)
    d_b = norm_back(d_act_b, hat_b, inverse_b, gain_b, shift_b_sum, gain_b_sum, total_count).astype(
        jnp.bfloat16
    )
    grad_wb = tdot(window_a, d_b)
    halo_d = padded(d_b.reshape(clip_dev, row_dev, col_count, d_mid), (("rows", 1),), 1)
    halo_d = jnp.pad(halo_d, ((0, 0), (0, 0), (1, 1), (0, 0)))
    window_d = jnp.concatenate(
        [
            halo_d[
                :, 2 - row_step : 2 - row_step + row_dev, 2 - col_step : 2 - col_step + col_count
            ]
            for row_step in range(3)
            for col_step in range(3)
        ],
        axis=3,
    ).reshape(cell_count, 9 * d_mid)
    flipped = w_b.reshape(9, d_mid, d_mid).transpose(0, 2, 1).reshape(9 * d_mid, d_mid)
    d_act_a = jnp.dot(window_d, flipped, preferred_element_type=jnp.float32) * silu_slope(act_a)
    shift_a_sum, gain_a_sum = segment_totals(d_act_a, hat_a)
    d_a = norm_back(d_act_a, hat_a, inverse_a, gain_a, shift_a_sum, gain_a_sum, total_count).astype(
        jnp.bfloat16
    )
    grad_wa = tdot(flat_x, d_a)
    grad_input = (ndot(d_a, w_a) + d_pre).astype(jnp.bfloat16).reshape(features.shape)
    partial_sums = (
        lax.psum_scatter(grad_wa, "rows", scatter_dimension=0, tiled=True),
        lax.psum_scatter(grad_wb, "rows", scatter_dimension=0, tiled=True),
        lax.psum_scatter(grad_wc, "rows", scatter_dimension=0, tiled=True),
        lax.psum_scatter(grad_wq, "rows", scatter_dimension=0, tiled=True),
        lax.psum_scatter(grad_wk, "rows", scatter_dimension=0, tiled=True),
        lax.psum_scatter(grad_wv, "rows", scatter_dimension=0, tiled=True),
        lax.psum_scatter(grad_wo, "rows", scatter_dimension=0, tiled=True),
        lax.psum_scatter(grad_wh, "rows", scatter_dimension=0, tiled=True),
    )
    finished = (
        lax.psum_scatter(
            partial_sums[0].astype(jnp.bfloat16), "batch", scatter_dimension=1, tiled=True
        ).astype(jnp.float32),
        lax.psum_scatter(
            partial_sums[1].astype(jnp.bfloat16), "batch", scatter_dimension=1, tiled=True
        ).astype(jnp.float32),
        lax.psum_scatter(
            partial_sums[2].astype(jnp.bfloat16), "batch", scatter_dimension=1, tiled=True
        ).astype(jnp.float32),
        lax.psum_scatter(
            partial_sums[3].astype(jnp.bfloat16), "batch", scatter_dimension=1, tiled=True
        ).astype(jnp.float32),
        lax.psum_scatter(
            partial_sums[4].astype(jnp.bfloat16), "batch", scatter_dimension=1, tiled=True
        ).astype(jnp.float32),
        lax.psum_scatter(
            partial_sums[5].astype(jnp.bfloat16), "batch", scatter_dimension=1, tiled=True
        ).astype(jnp.float32),
        lax.psum_scatter(
            partial_sums[6].astype(jnp.bfloat16), "batch", scatter_dimension=1, tiled=True
        ).astype(jnp.float32),
        lax.psum_scatter(
            partial_sums[7].astype(jnp.bfloat16), "batch", scatter_dimension=1, tiled=True
        ).astype(jnp.float32),
    )
    return (
        likely,
        grad_input,
        finished[0],
        finished[1],
        finished[2],
        finished[3],
        finished[4],
        finished[5],
        finished[6],
        finished[7],
        gain_a_sum,
        shift_a_sum,
        gain_b_sum,
        shift_b_sum,
        head_sums[1],
        head_sums[0],
        head_sums[2],
        head_sums[3],
        head_sums[4],
    )


def solution(mesh):
    return jax.shard_map(
        on_device,
        mesh=mesh,
        in_specs=(
            P("batch", "rows", None, None),
            P("rows", None),
            P("rows", None),
            P("rows", None),
            P("rows", None),
            P("rows", None),
            P("rows", None),
            P("rows", None),
            P("rows", None),
            P(),
            P(),
            P(),
            P(),
            P(),
            P(),
            P(),
            P(),
            P(),
            P(("batch", "rows"), None),
            P(("batch", "rows"), None),
            P(("batch", "rows"), None),
            P(("batch", "rows")),
            P(("batch", "rows"), None),
            P(("batch", "rows"), None),
            P(("batch", "rows")),
            P(("batch", "rows")),
            P(("batch", "rows"), None),
        ),
        out_specs=(
            P(("batch", "rows"), None),
            P("batch", "rows", None, None),
            P("rows", "batch"),
            P("rows", "batch"),
            P("rows", "batch"),
            P("rows", "batch"),
            P("rows", "batch"),
            P("rows", "batch"),
            P("rows", "batch"),
            P("rows", "batch"),
            P(),
            P(),
            P(),
            P(),
            P(),
            P(),
            P(),
            P(),
            P(),
        ),
        check_vma=False,
    )
```

profile of v0, /device:TPU:0, one launch (start us, length us, event | category | flops | bytes accessed | tf_op | source)
XLA Modules:
  0.0 1011.4 jit_solution(11663919438469440399)
XLA Ops:
  11.2 6.3 all-to-all-start
  19.9 21.7 %all-gather.10.cloned.1.call-done = bf16[2048,512]{1,0:T(8,128)(2,1)} async-done(((bf16[256,512]{1,0:T(8,128)(2,1)}), bf16[2048,512]{1,0:T(8,128)(2,1)}) %all-gather.10.cloned.1.call-update) | async-done | bytes 2097168 | tf_op jit(solution)/shard_map/all_gather | solution.py:113
  41.6 5.2 fusion.49
  46.9 42.2 %all-reduce.8 = (f32[512]{0:T(512)S(1)}, f32[512]{0:T(512)S(1)}) all-reduce(f32[512]{0:T(512)S(1)} %get-tuple-element.106, f32[512]{0:T(512)S(1)} %get-tuple-element.105), channel_id=1, replica_groups=mesh['batch'=4,'rows'=8] {'batch','rows'}, use_global_device_ids=true, to_apply=%region_3.0 | all-reduce | flops 1024 | bytes 8192 | tf_op jit(solution)/shard_map/psum | solution.py:63
  89.8 2.7 collective-permute-start
  97.0 39.7 %all_gather.39 = bf16[4096,80]{0,1:T(8,128)(2,1)} all-gather(bf16[512,80]{0,1:T(8,128)(2,1)S(1)} %copy-done.8), channel_id=1, replica_groups=mesh['batch'=4,'rows'=8] {'rows'}, dimensions={0}, use_global_device_ids=true | all-gather | bytes 737280 | tf_op jit(solution)/shard_map/all_gather | solution.py:120
  138.5 3.6 select_maximum_fusion.2
  142.2 1.9 fusion.52
  145.2 2.4 constant_dynamic-update-slice_fusion.7
  153.6 2.3 constant_dynamic-update-slice_fusion.1
  157.1 10.1 %fusion.48 = (f32[512]{0:T(512)S(1)}, f32[512]{0:T(512)S(1)}, f32[1024,512]{1,0:T(8,128)}) fusion(bf16[1024,4608]{1,0:T(8,128)(2,1)} %constant_dynamic-update-slice_fusion, bf16[4608,512]{1,0:T(8,128)(2,1)} %all-gather.12.cloned.1.call-done), kind=kOutput, calls=%fused_computation.239 | convolution fusion | flops 4833410048 | bytes 16257024 | tf_op jit(solution)/shard_map/dot_general | solution.py:138
  167.2 41.5 %all-reduce.7 = (f32[512]{0:T(512)S(1)}, f32[512]{0:T(512)S(1)}) all-reduce(f32[512]{0:T(512)S(1)} %get-tuple-element.104, f32[512]{0:T(512)S(1)} %get-tuple-element.103), channel_id=1, replica_groups=mesh['batch'=4,'rows'=8] {'batch','rows'}, use_global_device_ids=true, to_apply=%region_7.8 | all-reduce | flops 1024 | bytes 8192 | tf_op jit(solution)/shard_map/psum | solution.py:63
  208.9 8.2 fusion.45
  217.0 42.3 %all-reduce.6 = (f32[2048]{0:T(1024)S(1)}, f32[2048]{0:T(1024)S(1)}) all-reduce(f32[2048]{0:T(1024)S(1)} %get-tuple-element.98, f32[2048]{0:T(1024)S(1)} %get-tuple-element.97), channel_id=1, replica_groups=mesh['batch'=4,'rows'=8] {'batch','rows'}, use_global_device_ids=true, to_apply=%region_11.12 | all-reduce | flops 4096 | bytes 32768 | tf_op jit(solution)/shard_map/psum | solution.py:63
  259.8 10.3 %fusion.6 = bf16[8,8,2048]{2,1,0:T(8,128)(2,1)} fusion(bf16[1024,2048]{1,0:T(8,128)(2,1)} %bitcast.110, f32[2048]{0:T(1024)S(1)} %copy-done.116, f32[2048]{0:T(1024)S(1)} %get-tuple-element.197, f32[1024,2048]{1,0:T(8,128)} %get-tuple-element.207, f32[2048]{0:T(1024)S(1)} %get-tuple-element.198, f32[2048]{0:T(1024)S(1)} %copy-done.20, ...), kind=kOutput, calls=%fused_computation.27 | convolution fusion | flops 297140224 | bytes 12892160 | tf_op jit(solution)/shard_map/dot_general | solution.py:165
  270.1 3.4 all-to-all-start.1
  273.6 2.0 fusion.14
  275.5 15.3 %all-gather = bf16[8,10,512]{2,1,0:T(8,128)(2,1)S(1)} all-gather(bf16[1,10,512]{2,1,0:T(8,128)(2,1)S(1)} %fusion.14), channel_id=1, replica_groups=mesh['batch'=4,'rows'=8] {'rows'}, dimensions={0}, use_global_device_ids=true | all-gather | bytes 92160 | tf_op jit(solution)/shard_map/all_gather | solution.py:183
  290.9 2.0 fusion.15
  292.9 14.4 %all-gather.1 = bf16[8,10,512]{2,1,0:T(8,128)(2,1)S(1)} all-gather(bf16[1,10,512]{2,1,0:T(8,128)(2,1)S(1)} %fusion.15), channel_id=1, replica_groups=mesh['batch'=4,'rows'=8] {'rows'}, dimensions={0}, use_global_device_ids=true | all-gather | bytes 92160 | tf_op jit(solution)/shard_map/all_gather | solution.py:184
  308.6 2.1 convolution_convert_fusion
  311.4 2.4 fusion.3
  313.9 2.8 convert_reduce_fusion
  321.0 3.1 multiply_reduce_fusion.6
  324.8 2.7 fusion.58
  327.6 4.1 fusion.20
  332.2 16.3 %all_to_all.24 = bf16[8,10,1024]{2,1,0:T(8,128)(2,1)S(1)} all-to-all(bf16[8,10,1024]{2,1,0:T(8,128)(2,1)S(1)} %reshape.231), channel_id=1, replica_groups=mesh['batch'=4,'rows'=8] {'rows'}, dimensions={0} | all-to-all | bytes 327680 | tf_op jit(solution)/shard_map/all_to_all | solution.py:32
  348.6 2.7 convolution_bitcast_fusion.1
  351.4 2.7 convolution_bitcast_fusion
  354.7 3.0 fusion.4
  358.5 17.0 %all_to_all.25 = bf16[8,8,2048]{2,1,0:T(8,128)(2,1)S(1)} all-to-all(bf16[8,8,2048]{2,1,0:T(8,128)(2,1)S(1)} %bitcast_select_fusion), channel_id=1, replica_groups=mesh['batch'=4,'rows'=8] {'rows'}, dimensions={0} | all-to-all | bytes 524288 | tf_op jit(solution)/shard_map/all_to_all | solution.py:242
  375.9 14.8 %fusion.44 = (f32[2048]{0:T(1024)S(1)}, f32[2048]{0:T(1024)S(1)}, f32[1024,2048]{1,0:T(8,128)}) fusion(f32[2048]{0:T(1024)S(1)} %get-tuple-element.197, f32[1024,2048]{1,0:T(8,128)} %get-tuple-element.207, f32[2048]{0:T(1024)S(1)} %get-tuple-element.198, bf16[1024,2048]{1,0:T(8,128)(2,1)} %bitcast.111, f32[2048]{0:T(1024)} %param.41, ...), kind=kOutput, calls=%fused_computation.235 | convolution fusion | flops 309587968 | bytes 21297152 | tf_op jit(solution)/shard_map/dot_general | solution.py:46
  390.7 38.9 %all-reduce.5 = (f32[2048]{0:T(1024)S(1)}, f32[2048]{0:T(1024)S(1)}) all-reduce(f32[2048]{0:T(1024)S(1)} %get-tuple-element.96, f32[2048]{0:T(1024)S(1)} %get-tuple-element.95), channel_id=1, replica_groups=mesh['batch'=4,'rows'=8] {'batch','rows'}, use_global_device_ids=true, to_apply=%region_22.23 | all-reduce | flops 4096 | bytes 32768 | tf_op jit(solution)/shard_map/psum | solution.py:245
  429.7 7.4 multiply_convert_fusion
  437.1 2.0 copy-done.6
  439.2 4.6 fusion.42
  444.0 8.1 fusion.47
  452.1 42.8 %all-reduce.4 = (f32[512]{0:T(512)S(1)}, f32[512]{0:T(512)S(1)}) all-reduce(f32[512]{0:T(512)S(1)} %get-tuple-element.102, f32[512]{0:T(512)S(1)} %get-tuple-element.101), channel_id=1, replica_groups=mesh['batch'=4,'rows'=8] {'batch','rows'}, use_global_device_ids=true, to_apply=%region_26.27 | all-reduce | flops 1024 | bytes 8192 | tf_op jit(solution)/shard_map/psum | solution.py:70
  494.8 2.9 multiply_convert_fusion.8
  497.7 2.7 collective-permute-start.2
  501.7 6.7 copy.62
  508.4 3.6 select_maximum_fusion
  512.1 1.9 fusion.51
  518.0 7.1 fusion.46
  525.2 53.3 %all-reduce.3 = (f32[512]{0:T(512)S(1)}, f32[512]{0:T(512)S(1)}, f32[512]{0:T(512)}, f32[512]{0:T(512)}, f32[80]{0:T(128)}) all-reduce(f32[512]{0:T(512)S(1)} %get-tuple-element.100, f32[512]{0:T(512)S(1)} %get-tuple-element.99, f32[512]{0:T(512)S(1)} %copy-done.28, ...), channel_id=1, replica_groups=mesh['batch'=4,'rows'=8] {'batch','rows'}, use_global_device_ids=true, to_apply=%region_30.31 | all-reduce | flops 2128 | bytes 17024 | tf_op jit(solution)/shard_map/psum | solution.py:70
  578.4 2.4 multiply_convert_fusion.7
  581.8 4.4 convolution_bitcast_fusion.2
  586.3 11.4 %fusion.57 = f32[4608,512]{1,0:T(8,128)} fusion(bf16[1024,4608]{1,0:T(8,128)(2,1)} %constant_dynamic-update-slice_fusion, bf16[1024,512]{1,0:T(8,128)(2,1)S(1)} %multiply_convert_fusion.8), kind=kOutput, calls=%fused_computation.247 | convolution fusion | flops 4831838208 | bytes 19922944 | tf_op jit(solution)/shard_map/dot_general | solution.py:46
  601.5 1.8 convert_element_type.180
  603.4 1.9 convert_element_type.176
  607.2 10.4 %reduce-scatter.26.cloned.1.call-done = f32[64,2048]{1,0:T(8,128)} async-done(((f32[512,2048]{1,0:T(8,128)}), f32[64,2048]{1,0:T(8,128)}) %reduce-scatter.26.cloned.1.call-update) | async-done | bytes 524304 | tf_op jit(solution)/shard_map/reduce_scatter | solution.py:282
  617.6 1.8 convert_element_type.169
  619.5 49.1 %reduce-scatter.20.cloned.1.call-done = f32[256,512]{0,1:T(8,128)} async-done(((f32[2048,512]{0,1:T(8,128)}), f32[256,512]{0,1:T(8,128)}) %reduce-scatter.20.cloned.1.call-update) | async-done | bytes 524304 | tf_op jit(solution)/shard_map/reduce_scatter | solution.py:280
  668.6 1.8 convert_element_type.165
  670.4 98.0 %reduce-scatter.24.cloned.1.call-done = f32[576,512]{1,0:T(8,128)} async-done(((f32[4608,512]{1,0:T(8,128)}), f32[576,512]{1,0:T(8,128)}) %reduce-scatter.24.cloned.1.call-update) | async-done | bytes 1179664 | tf_op jit(solution)/shard_map/reduce_scatter | solution.py:281
  772.2 8.5 add_convert_fusion
  780.7 30.6 %all-reduce.11.cloned.1.call-done = bf16[512,80]{0,1:T(8,128)(2,1)} async-done(((bf16[512,80]{0,1:T(8,128)(2,1)}), bf16[512,80]{0,1:T(8,128)(2,1)}) %all-reduce.11.cloned.1.call-update) | async-done | bytes 81936
  812.6 26.3 %reduce-scatter.48.cloned.1.call-done = bf16[128,256]{1,0:T(8,128)(2,1)} async-done(((bf16[512,256]{1,0:T(8,128)(2,1)}), bf16[128,256]{1,0:T(8,128)(2,1)}) %reduce-scatter.48.cloned.1.call-update) | async-done | bytes 65552
  840.5 25.1 %reduce-scatter.42.cloned.1.call-done = bf16[64,512]{1,0:T(8,128)(2,1)} async-done(((bf16[64,2048]{1,0:T(8,128)(2,1)}), bf16[64,512]{1,0:T(8,128)(2,1)}) %reduce-scatter.42.cloned.1.call-update) | async-done | bytes 65552 | tf_op jit(solution)/shard_map/reduce_scatter | solution.py:308
  867.2 25.6 %reduce-scatter.34.cloned.1.call-done = bf16[256,128]{0,1:T(8,128)(2,1)} async-done(((bf16[256,512]{0,1:T(8,128)(2,1)}), bf16[256,128]{0,1:T(8,128)(2,1)}) %reduce-scatter.34.cloned.1.call-update) | async-done | bytes 65552 | tf_op jit(solution)/shard_map/reduce_scatter | solution.py:302
  894.4 25.1 %reduce-scatter.38.cloned.1.call-done = bf16[256,128]{0,1:T(8,128)(2,1)} async-done(((bf16[256,512]{0,1:T(8,128)(2,1)}), bf16[256,128]{0,1:T(8,128)(2,1)}) %reduce-scatter.38.cloned.1.call-update) | async-done | bytes 65552 | tf_op jit(solution)/shard_map/reduce_scatter | solution.py:305
  921.1 25.5 %reduce-scatter.28.cloned.1.call-done = bf16[64,512]{1,0:T(8,128)(2,1)} async-done(((bf16[64,2048]{1,0:T(8,128)(2,1)}), bf16[64,512]{1,0:T(8,128)(2,1)}) %reduce-scatter.28.cloned.1.call-update) | async-done | bytes 65552 | tf_op jit(solution)/shard_map/reduce_scatter | solution.py:296
  948.1 26.0 %reduce-scatter.22.cloned.1.call-done = bf16[256,128]{0,1:T(8,128)(2,1)} async-done(((bf16[256,512]{0,1:T(8,128)(2,1)}), bf16[256,128]{0,1:T(8,128)(2,1)}) %reduce-scatter.22.cloned.1.call-update) | async-done | bytes 65552 | tf_op jit(solution)/shard_map/reduce_scatter | solution.py:290
  975.6 27.0 %reduce-scatter.46.cloned.1.call-done = bf16[128,576]{1,0:T(8,128)(2,1)} async-done(((bf16[512,576]{1,0:T(8,128)(2,1)}), bf16[128,576]{1,0:T(8,128)(2,1)}) %reduce-scatter.46.cloned.1.call-update) | async-done | bytes 147472
  (396 shorter events, 58.3 us)
Async XLA Ops:
  7.2 266.4 %copy-start = (bf16[10,2048]{1,0:T(8,128)(2,1)S(1)}, bf16[10,2048]{1,0:T(8,128)(2,1)}, u32[]{:S(2)}) copy-start(bf16[10,2048]{1,0:T(8,128)(2,1)} %param.45) | copy-start | bytes 122884
  7.2 34.4 %all-gather.10.cloned.1.call-start = ((), (), s32[]{:S(2)}) async-start(), calls=%async_computation.19 | async-start | bytes 2359296 | tf_op jit(solution)/shard_map/all_gather | solution.py:113
  7.9 149.2 %all-gather.12.cloned.1.call-start = ((), (), s32[]{:S(2)}) async-start(), calls=%async_computation.20 | async-start | bytes 5308416 | tf_op jit(solution)/shard_map/all_gather | solution.py:114
  8.7 200.1 %all-gather.14.cloned.1.call-start = ((), (), s32[]{:S(2)}) async-start(), calls=%async_computation.21 | async-start | bytes 2359296 | tf_op jit(solution)/shard_map/all_gather | solution.py:115
  9.4 264.1 %all-gather.18.cloned.1.call-start = ((), (), s32[]{:S(2)}) async-start(), calls=%async_computation.23 | async-start | bytes 2359296 | tf_op jit(solution)/shard_map/all_gather | solution.py:117
  10.0 280.9 %all-gather.20.cloned.1.call-start = ((), (), s32[]{:S(2)}) async-start(), calls=%async_computation.24 | async-start | bytes 2359296 | tf_op jit(solution)/shard_map/all_gather | solution.py:118
  10.6 298.0 %all-gather.16.cloned.1.call-start = ((), (), s32[]{:S(2)}) async-start(), calls=%async_computation.22 | async-start | bytes 2359296 | tf_op jit(solution)/shard_map/all_gather | solution.py:116
  11.2 126.1 %all-to-all-start = ((s32[8,1,8]{2,1,0:T(1,128)}), s32[8,1,8]{2,1,0:T(1,128)S(1)}, u32[]{:S(2)}, u32[]{:S(2)}) async-start(s32[8,1,8]{2,1,0:T(1,128)} %bitcast.138), calls=%async_computation | async-start | bytes 8192 | tf_op jit(solution)/shard_map/all_to_all | solution.py:171
  17.5 293.9 %all-gather.22.cloned.1.call-start = ((), (), s32[]{:S(2)}) async-start(), calls=%async_computation.25 | async-start | bytes 2359296 | tf_op jit(solution)/shard_map/all_gather | solution.py:119
  89.8 48.7 %collective-permute-start = (bf16[64,1,16,512]{3,2,0,1:T(8,128)(2,1)S(1)}, bf16[64,1,16,512]{3,2,0,1:T(8,128)(2,1)}, u32[]{:S(2)}, u32[]{:S(2)}) collective-permute-start(bf16[64,1,16,512]{3,2,0,1:T(8,128)(2,1)S(1)} %bitcast.117), channel_id=1, source_target_pairs={{0,1},{1,2},{2,3},{3,4},{4,5},{5,6},{6,7},{8,9},{9,10},{10,11},{11... | collective-permute-start | bytes 3145736 | tf_op jit(solution)/shard_map/ppermute | solution.py:15
  92.5 46.0 %collective-permute-start.1 = (bf16[64,1,16,512]{3,2,0,1:T(8,128)(2,1)S(1)}, bf16[64,1,16,512]{3,2,0,1:T(8,128)(2,1)}, u32[]{:S(2)}, u32[]{:S(2)}) collective-permute-start(bf16[64,1,16,512]{3,2,0,1:T(8,128)(2,1)S(1)} %bitcast.118), channel_id=1, source_target_pairs={{1,0},{2,1},{3,2},{4,3},{5,4},{6,5},{7,6},{9,8},{10,9},{11,10},{12... | collective-permute-start | bytes 3145736 | tf_op jit(solution)/shard_map/ppermute | solution.py:17
  94.4 165.0 %copy-start.35 = (s32[64]{0:T(128)}, s32[64]{0:T(128)S(1)}, u32[]{:S(2)}) copy-start(s32[64]{0:T(128)S(1)} %get-tuple-element.149) | copy-start | bytes 772
  94.4 165.0 %copy-start.37 = (s32[64]{0:T(128)}, s32[64]{0:T(128)S(1)}, u32[]{:S(2)}) copy-start(s32[64]{0:T(128)S(1)} %get-tuple-element.150) | copy-start | bytes 772
  94.4 165.0 %copy-start.39 = (s32[64]{0:T(128)}, s32[64]{0:T(128)S(1)}, u32[]{:S(2)}) copy-start(s32[64]{0:T(128)S(1)} %get-tuple-element.151) | copy-start | bytes 772
  94.4 165.0 %copy-start.41 = (s32[64]{0:T(128)}, s32[64]{0:T(128)S(1)}, u32[]{:S(2)}) copy-start(s32[64]{0:T(128)S(1)} %get-tuple-element.152) | copy-start | bytes 772
  94.4 165.0 %copy-start.43 = (s32[64]{0:T(128)}, s32[64]{0:T(128)S(1)}, u32[]{:S(2)}) copy-start(s32[64]{0:T(128)S(1)} %get-tuple-element.153) | copy-start | bytes 772
  94.5 165.0 %copy-start.45 = (s32[64]{0:T(128)}, s32[64]{0:T(128)S(1)}, u32[]{:S(2)}) copy-start(s32[64]{0:T(128)S(1)} %get-tuple-element.154) | copy-start | bytes 772
  94.5 165.0 %copy-start.47 = (s32[64]{0:T(128)}, s32[64]{0:T(128)S(1)}, u32[]{:S(2)}) copy-start(s32[64]{0:T(128)S(1)} %get-tuple-element.155) | copy-start | bytes 772
  94.5 165.0 %copy-start.49 = (s32[64]{0:T(128)}, s32[64]{0:T(128)S(1)}, u32[]{:S(2)}) copy-start(s32[64]{0:T(128)S(1)} %get-tuple-element.156) | copy-start | bytes 772
  94.5 165.0 %copy-start.51 = (s32[64]{0:T(128)}, s32[64]{0:T(128)S(1)}, u32[]{:S(2)}) copy-start(s32[64]{0:T(128)S(1)} %get-tuple-element.157) | copy-start | bytes 772
  95.7 163.8 %copy-start.73 = (s32[64]{0:T(128)}, s32[64]{0:T(128)S(1)}, u32[]{:S(2)}) copy-start(s32[64]{0:T(128)S(1)} %get-tuple-element.111) | copy-start | bytes 772
  95.7 163.8 %copy-start.75 = (s32[64]{0:T(128)}, s32[64]{0:T(128)S(1)}, u32[]{:S(2)}) copy-start(s32[64]{0:T(128)S(1)} %get-tuple-element.112) | copy-start | bytes 772
  95.7 163.8 %copy-start.77 = (s32[64]{0:T(128)}, s32[64]{0:T(128)S(1)}, u32[]{:S(2)}) copy-start(s32[64]{0:T(128)S(1)} %get-tuple-element.113) | copy-start | bytes 772
  95.7 163.8 %copy-start.79 = (s32[64]{0:T(128)}, s32[64]{0:T(128)S(1)}, u32[]{:S(2)}) copy-start(s32[64]{0:T(128)S(1)} %get-tuple-element.114) | copy-start | bytes 772
  95.7 163.8 %copy-start.81 = (s32[64]{0:T(128)}, s32[64]{0:T(128)S(1)}, u32[]{:S(2)}) copy-start(s32[64]{0:T(128)S(1)} %get-tuple-element.115) | copy-start | bytes 772
  95.7 163.9 %copy-start.83 = (s32[64]{0:T(128)}, s32[64]{0:T(128)S(1)}, u32[]{:S(2)}) copy-start(s32[64]{0:T(128)S(1)} %get-tuple-element.116) | copy-start | bytes 772
  95.7 163.9 %copy-start.85 = (s32[64]{0:T(128)}, s32[64]{0:T(128)S(1)}, u32[]{:S(2)}) copy-start(s32[64]{0:T(128)S(1)} %get-tuple-element.117) | copy-start | bytes 772
  95.7 163.9 %copy-start.87 = (s32[64]{0:T(128)}, s32[64]{0:T(128)S(1)}, u32[]{:S(2)}) copy-start(s32[64]{0:T(128)S(1)} %get-tuple-element.118) | copy-start | bytes 772
  95.7 163.9 %copy-start.89 = (s32[64]{0:T(128)}, s32[64]{0:T(128)S(1)}, u32[]{:S(2)}) copy-start(s32[64]{0:T(128)S(1)} %get-tuple-element.119) | copy-start | bytes 772
  95.7 163.9 %copy-start.91 = (s32[64]{0:T(128)}, s32[64]{0:T(128)S(1)}, u32[]{:S(2)}) copy-start(s32[64]{0:T(128)S(1)} %get-tuple-element.120) | copy-start | bytes 772
  95.7 163.9 %copy-start.93 = (s32[64]{0:T(128)}, s32[64]{0:T(128)S(1)}, u32[]{:S(2)}) copy-start(s32[64]{0:T(128)S(1)} %get-tuple-element.121) | copy-start | bytes 772
  95.7 163.9 %copy-start.95 = (s32[64]{0:T(128)}, s32[64]{0:T(128)S(1)}, u32[]{:S(2)}) copy-start(s32[64]{0:T(128)S(1)} %get-tuple-element.122) | copy-start | bytes 772
  95.8 163.9 %copy-start.97 = (s32[64]{0:T(128)}, s32[64]{0:T(128)S(1)}, u32[]{:S(2)}) copy-start(s32[64]{0:T(128)S(1)} %get-tuple-element.123) | copy-start | bytes 772
  95.8 163.9 %copy-start.99 = (s32[64]{0:T(128)}, s32[64]{0:T(128)S(1)}, u32[]{:S(2)}) copy-start(s32[64]{0:T(128)S(1)} %get-tuple-element.124) | copy-start | bytes 772
  95.8 163.9 %copy-start.101 = (s32[64]{0:T(128)}, s32[64]{0:T(128)S(1)}, u32[]{:S(2)}) copy-start(s32[64]{0:T(128)S(1)} %get-tuple-element.125) | copy-start | bytes 772
  95.8 163.9 %copy-start.103 = (s32[64]{0:T(128)}, s32[64]{0:T(128)S(1)}, u32[]{:S(2)}) copy-start(s32[64]{0:T(128)S(1)} %get-tuple-element.126) | copy-start | bytes 772
  95.8 163.9 %copy-start.105 = (s32[64]{0:T(128)}, s32[64]{0:T(128)S(1)}, u32[]{:S(2)}) copy-start(s32[64]{0:T(128)S(1)} %get-tuple-element.127) | copy-start | bytes 772
  97.0 162.6 %copy-start.111 = (f32[64]{0:T(128)}, f32[64]{0:T(128)S(1)}, u32[]{:S(2)}) copy-start(f32[64]{0:T(128)S(1)} %get-tuple-element.130) | copy-start | bytes 772
  97.0 162.6 %copy-start.113 = (f32[64]{0:T(128)}, f32[64]{0:T(128)S(1)}, u32[]{:S(2)}) copy-start(f32[64]{0:T(128)S(1)} %get-tuple-element.131) | copy-start | bytes 772
  137.1 122.5 %copy-start.53 = (f32[64]{0:T(128)}, f32[64]{0:T(128)S(1)}, u32[]{:S(2)}) copy-start(f32[64]{0:T(128)S(1)} %get-tuple-element.158) | copy-start | bytes 772
  137.2 122.5 %copy-start.55 = (f32[64]{0:T(128)}, f32[64]{0:T(128)S(1)}, u32[]{:S(2)}) copy-start(f32[64]{0:T(128)S(1)} %get-tuple-element.159) | copy-start | bytes 772
  137.2 122.5 %copy-start.57 = (f32[64]{0:T(128)}, f32[64]{0:T(128)S(1)}, u32[]{:S(2)}) copy-start(f32[64]{0:T(128)S(1)} %get-tuple-element.160) | copy-start | bytes 772
  270.1 37.2 %all-to-all-start.1 = ((bf16[8,8,2048]{2,1,0:T(8,128)(2,1)}), bf16[8,8,2048]{2,1,0:T(8,128)(2,1)S(1)}, u32[]{:S(2)}, u32[]{:S(2)}) async-start(bf16[8,8,2048]{2,1,0:T(8,128)(2,1)} %fusion.6), calls=%async_computation.1 | async-start | bytes 524288 | tf_op jit(solution)/shard_map/all_to_all | solution.py:170
  273.5 324.3 %reduce-scatter.44.cloned.1.call-start = ((), (), s32[]{:S(2)}) async-start(), calls=%async_computation.38 | async-start | bytes 1474560 | tf_op jit(solution)/shard_map/reduce_scatter | solution.py:287
  318.1 281.4 %reduce-scatter.30.cloned.1.call-start = ((), (), s32[]{:S(2)}) async-start(), calls=%async_computation.31 | async-start | bytes 4718592 | tf_op jit(solution)/shard_map/reduce_scatter | solution.py:283
  327.5 274.0 %reduce-scatter.40.cloned.1.call-start = ((), (), s32[]{:S(2)}) async-start(), calls=%async_computation.36 | async-start | bytes 4718592 | tf_op jit(solution)/shard_map/reduce_scatter | solution.py:286
  331.8 271.6 %reduce-scatter.32.cloned.1.call-start = ((), (), s32[]{:S(2)}) async-start(), calls=%async_computation.32 | async-start | bytes 4718592 | tf_op jit(solution)/shard_map/reduce_scatter | solution.py:284
  351.4 254.0 %reduce-scatter.36.cloned.1.call-start = ((), (), s32[]{:S(2)}) async-start(), calls=%async_computation.34 | async-start | bytes 4718592 | tf_op jit(solution)/shard_map/reduce_scatter | solution.py:285
  354.5 263.1 %reduce-scatter.26.cloned.1.call-start = ((), (), s32[]{:S(2)}) async-start(), calls=%async_computation.29 | async-start | bytes 4718592 | tf_op jit(solution)/shard_map/reduce_scatter | solution.py:282
  443.7 224.8 %reduce-scatter.20.cloned.1.call-start = ((), (), s32[]{:S(2)}) async-start(), calls=%async_computation.26 | async-start | bytes 4718592 | tf_op jit(solution)/shard_map/reduce_scatter | solution.py:280
  497.7 10.7 %collective-permute-start.2 = (bf16[64,1,16,512]{3,2,0,1:T(8,128)(2,1)S(1)}, bf16[64,1,16,512]{3,2,0,1:T(8,128)(2,1)}, u32[]{:S(2)}, u32[]{:S(2)}) collective-permute-start(bf16[64,1,16,512]{3,2,0,1:T(8,128)(2,1)S(1)} %bitcast.106), channel_id=1, source_target_pairs={{0,1},{1,2},{2,3},{3,4},{4,5},{5,6},{6,7},{8,9},{9,10},{10,11},{11... | collective-permute-start | bytes 3145736 | tf_op jit(solution)/shard_map/ppermute | solution.py:15
  500.4 8.0 collective-permute-start.3
  586.3 182.1 %reduce-scatter.24.cloned.1.call-start = ((), (), s32[]{:S(2)}) async-start(), calls=%async_computation.28 | async-start | bytes 10616832 | tf_op jit(solution)/shard_map/reduce_scatter | solution.py:281
  597.8 213.5 %all-reduce.11.cloned.1.call-start = ((), (), s32[]{:S(2)}) async-start(), calls=%async_computation.41 | async-start | bytes 163840
  599.4 239.5 %reduce-scatter.48.cloned.1.call-start = ((), (), s32[]{:S(2)}) async-start(), calls=%async_computation.40 | async-start | bytes 327680
  601.4 264.2 %reduce-scatter.42.cloned.1.call-start = ((), (), s32[]{:S(2)}) async-start(), calls=%async_computation.37 | async-start | bytes 327680 | tf_op jit(solution)/shard_map/reduce_scatter | solution.py:308
  603.3 167.6 %copy-start.121 = (u32[32]{0:T(128)S(1)}, u32[32]{0:T(128)}, u32[]{:S(2)}) copy-start(u32[32]{0:T(128)} %constant.85) | copy-start | bytes 388
  603.3 168.8 %copy-start.5 = (bf16[1024,512]{1,0:T(8,128)(2,1)S(1)}, bf16[1024,512]{1,0:T(8,128)(2,1)}, u32[]{:S(2)}) copy-start(bf16[1024,512]{1,0:T(8,128)(2,1)} %copy-done.4) | copy-start | bytes 3145732
  603.3 289.4 %reduce-scatter.34.cloned.1.call-start = ((), (), s32[]{:S(2)}) async-start(), calls=%async_computation.33 | async-start | bytes 327680 | tf_op jit(solution)/shard_map/reduce_scatter | solution.py:302
  605.3 314.1 %reduce-scatter.38.cloned.1.call-start = ((), (), s32[]{:S(2)}) async-start(), calls=%async_computation.35 | async-start | bytes 327680 | tf_op jit(solution)/shard_map/reduce_scatter | solution.py:305
  607.2 339.4 %reduce-scatter.28.cloned.1.call-start = ((), (), s32[]{:S(2)}) async-start(), calls=%async_computation.30 | async-start | bytes 327680 | tf_op jit(solution)/shard_map/reduce_scatter | solution.py:296
  619.4 354.6 %reduce-scatter.22.cloned.1.call-start = ((), (), s32[]{:S(2)}) async-start(), calls=%async_computation.27 | async-start | bytes 327680 | tf_op jit(solution)/shard_map/reduce_scatter | solution.py:290
  670.3 332.3 %reduce-scatter.46.cloned.1.call-start = ((), (), s32[]{:S(2)}) async-start(), calls=%async_computation.39 | async-start | bytes 819200
  772.1 232.3 %copy-start.1 = (bf16[10,2048]{1,0:T(8,128)(2,1)S(1)}, bf16[10,2048]{1,0:T(8,128)(2,1)}, u32[]{:S(2)}) copy-start(bf16[10,2048]{1,0:T(8,128)(2,1)} %param.45) | copy-start | bytes 122884
  (89 other events, 2596.5 us)
Sparse Core Ops, SparseCore 0:
  9.6 31.8 all-gather.9
  43.2 51.9 all-gather.11
  96.8 35.5 all-gather.13
  133.9 28.7 all-gather.17
  164.2 29.0 all-gather.19
  194.7 28.8 all-gather.15
  225.2 29.4 all-gather.21
  318.2 34.8 reduce-scatter.43
  355.4 53.8 reduce-scatter.29
  411.4 49.2 reduce-scatter.39
  463.0 51.3 reduce-scatter.31
  516.6 50.5 reduce-scatter.35
  569.4 48.1 reduce-scatter.25
  620.4 48.1 reduce-scatter.19
  670.7 97.6 reduce-scatter.23
  771.7 39.4 all-reduce.10
  814.1 24.8 reduce-scatter.47
  841.5 24.0 reduce-scatter.41
  868.6 24.0 reduce-scatter.33
  895.4 24.0 reduce-scatter.37
  922.4 24.0 reduce-scatter.27
  949.9 24.0 reduce-scatter.21
  977.2 25.3 reduce-scatter.45
where the time goes:
time: 1020 us; the launch traced here: 1010 us
  waiting for transfers between devices  395 us (39%)
  blocking collectives  364 us (36%)
  matrix products  128 us (13%)
  local copies, waits for them, and re-layouts  45.6 us (4%)
  other arithmetic  43.2 us (4%)
  starting transfers between devices  18.9 us (2%)
  between operations  17.1 us (2%)
    psum x3, blocking collectives, normalize(): lax.psum((jnp.sum(field, 0), jnp.sum(field * field, 0)), ('batch', 'rows'))  126 us
    reduce_scatter x1, waiting for transfers between devices, on_device(): lax.psum_scatter(grad_wb, 'rows', scatter_dimension=0, tiled=True)  98 us
    psum x2, blocking collectives, segment_totals(): lax.psum((jnp.sum(grad, 0), jnp.sum(grad * normed, 0)), ('batch', 'rows'))  96 us
    unnamed x26, waiting for transfers between devices  88.4 us
    dot_general x11, matrix products, tdot(): lax.dot_general(left, right, (((0,), (0,)), ((), ())), preferred_element_...  49.2 us
    reduce_scatter x1, waiting for transfers between devices, on_device(): lax.psum_scatter(grad_wa, 'rows', scatter_dimension=0, tiled=True)  49.1 us
    all_gather x1, blocking collectives, on_device(): lax.all_gather(w_head, 'rows', axis=0, tiled=True)  39.7 us
    psum x1, blocking collectives, on_device(): lax.psum((jnp.sum(d_pre, 0), jnp.sum(d_pre * hat_c, 0), grad_ln_gain, gra...  38.9 us
  transfers between devices with their start and end apart: 29, of which 12 were waited for; matrix products, arithmetic and copies ran while one was open for 20% of the time, Pallas kernels for 0%

commit v1 on v0

--- a/solution.py
+++ b/solution.py
@@ -109,8 +109,28 @@
     clip_dev, row_dev, col_count, d_in = features.shape
     cell_count = clip_dev * row_dev * col_count
     total_count = cell_count * owners * lax.axis_size("batch")
+
+    def track_rounds(u):
+        named_axis = "rows"
+        high, moved, later = (lax.axis_size(named_axis), lax.axis_index(named_axis), u.shape[0])
+        q_next, a_now = (u, 1)
+        while a_now < high:
+            q_next = jnp.concatenate(
+                [
+                    q_next,
+                    lax.ppermute(
+                        q_next,
+                        axis_name=named_axis,
+                        perm=list(map(lambda ix: (ix, (ix - a_now) % high), range(high))),
+                    ),
+                ],
+                0,
+            )
+            a_now = 2 * a_now
+        return jnp.roll(q_next, moved * later, 0)
+
     w_a, w_b, w_c, w_q, w_k, w_v, w_o, w_h = (
-        lax.all_gather(w_reduce, "rows", axis=0, tiled=True),
+        track_rounds(w_reduce),
         lax.all_gather(w_spatial, "rows", axis=0, tiled=True),
         lax.all_gather(w_expand, "rows", axis=0, tiled=True),
         lax.all_gather(query_weight, "rows", axis=0, tiled=True),

time: 1020 us -> 1120 us (1.098)
  local copies, waits for them, and re-layouts: 45.6 us -> 95.2 us
  waiting for transfers between devices: 395 us -> 441 us
    ppermute x0 -> x3, waiting for transfers between devices: none -> 93.2 us  [track_rounds(): lax.ppermute(q_next, axis_name=named_axis, perm=list(map(lambda ix: (ix,...]
    all_gather x1 -> x0, waiting for transfers between devices: 21.7 us -> none  [on_device(): lax.all_gather(w_reduce, 'rows', axis=0, tiled=True)]
    concatenate x1 -> x9, local copies, waits for them, and re-layouts: 0.07 us -> 18.5 us  [on_device(): jnp.concatenate([halo_d[:, 2 - row_step:2 - row_step + row_dev, 2 - col_s...]
    concatenate x1 -> x9, local copies, waits for them, and re-layouts: 1.15 us -> 18.6 us  [on_device(): jnp.concatenate([halo_a[:, row_step:row_step + row_dev, col_step:col_step...]
    reduce_scatter x1, waiting for transfers between devices: 49.1 us -> 36.1 us  [on_device(): lax.psum_scatter(grad_wa, 'rows', scatter_dimension=0, tiled=True)]
    unnamed x273 -> x334, local copies, waits for them, and re-layouts: 28.3 us -> 33.3 us
    unnamed x26 -> x25, waiting for transfers between devices: 88.4 us -> 86.5 us
  transfers between devices with their start and end apart: 29 -> 31, of which waited for: 12 -> 13; matrix products, arithmetic and copies ran while one was open for 20% -> 23% of each run, Pallas kernels for 0% -> 0%
where the time goes in v1:
time: 1120 us; the launch traced here: 1110 us
  waiting for transfers between devices  441 us (39%)
  blocking collectives  361 us (32%)
  matrix products  129 us (12%)
  local copies, waits for them, and re-layouts  95.2 us (8%)
  other arithmetic  43.2 us (4%)
  starting transfers between devices  21.9 us (2%)
  between operations  17.7 us (2%)
    psum x3, blocking collectives, normalize(): lax.psum((jnp.sum(field, 0), jnp.sum(field * field, 0)), ('batch', 'rows'))  123 us
    reduce_scatter x1, waiting for transfers between devices, on_device(): lax.psum_scatter(grad_wb, 'rows', scatter_dimension=0, tiled=True)  98 us
    psum x2, blocking collectives, segment_totals(): lax.psum((jnp.sum(grad, 0), jnp.sum(grad * normed, 0)), ('batch', 'rows'))  94 us
    ppermute x3, waiting for transfers between devices, track_rounds(): lax.ppermute(q_next, axis_name=named_axis, perm=list(map(lambda ix: (ix,...  93.2 us
    unnamed x25, waiting for transfers between devices  86.5 us
    dot_general x11, matrix products, tdot(): lax.dot_general(left, right, (((0,), (0,)), ((), ())), preferred_element_...  52.6 us
    all_gather x1, blocking collectives, on_device(): lax.all_gather(w_head, 'rows', axis=0, tiled=True)  42.6 us
    psum x1, blocking collectives, on_device(): lax.psum((jnp.sum(d_pre, 0), jnp.sum(d_pre * hat_c, 0), grad_ln_gain, gra...  39.1 us
  transfers between devices with their start and end apart: 31, of which 13 were waited for; matrix products, arithmetic and copies ran while one was open for 23% of the time, Pallas kernels for 0%

profile of v1, /device:TPU:0, one launch (start us, length us, event | category | flops | bytes accessed | tf_op | source)
XLA Modules:
  0.0 1110.0 jit_solution(3203136915428644195)
XLA Ops:
  10.6 4.5 collective-permute-start
  15.2 4.2 collective-permute-done
  21.0 35.9 %collective-permute-done.1 = bf16[512,512]{1,0:T(8,128)(2,1)S(1)} collective-permute-done((bf16[512,512]{1,0:T(8,128)(2,1)S(1)}, bf16[512,512]{1,0:T(8,128)(2,1)S(1)}, u32[]{:S(2)}, u32[]{:S(2)}) %collective-permute-start.1) | collective-permute-done | bytes 524320 | tf_op jit(solution)/shard_map/ppermute | solution.py:121
  57.9 4.2 all-to-all-start
  63.1 53.1 %collective-permute-done.2 = bf16[1024,512]{1,0:T(8,128)(2,1)S(1)} collective-permute-done((bf16[1024,512]{1,0:T(8,128)(2,1)S(1)}, bf16[1024,512]{1,0:T(8,128)(2,1)S(1)}, u32[]{:S(2)}, u32[]{:S(2)}) %collective-permute-start.2) | collective-permute-done | bytes 1048608 | tf_op jit(solution)/shard_map/ppermute | solution.py:121
  116.5 2.5 fusion.62
  119.0 42.5 %all-reduce.8 = (f32[512]{0:T(512)S(1)}, f32[512]{0:T(512)S(1)}) all-reduce(f32[512]{0:T(512)S(1)} %get-tuple-element.106, f32[512]{0:T(512)S(1)} %get-tuple-element.105), channel_id=1, replica_groups=mesh['batch'=4,'rows'=8] {'batch','rows'}, use_global_device_ids=true, to_apply=%region_3.4 | all-reduce | flops 1024 | bytes 8192 | tf_op jit(solution)/shard_map/psum | solution.py:63
  164.3 2.7 collective-permute-start.3
  171.5 42.6 %all_gather.35 = bf16[4096,80]{0,1:T(8,128)(2,1)} all-gather(bf16[512,80]{0,1:T(8,128)(2,1)S(1)} %copy-done.16), channel_id=1, replica_groups=mesh['batch'=4,'rows'=8] {'rows'}, dimensions={0}, use_global_device_ids=true | all-gather | bytes 737280 | tf_op jit(solution)/shard_map/all_gather | solution.py:140
  215.8 3.6 select_maximum_fusion.2
  219.5 4.1 fusion.65
  228.2 2.3 copy.109
  235.0 2.4 constant_dynamic-update-slice_fusion.15
  244.9 2.3 copy.113
  248.5 2.4 copy.115
  250.9 2.4 constant_dynamic-update-slice_fusion.11
  257.8 10.1 fusion.61
  267.9 2.9 copy.116
  270.8 38.9 %all-reduce.7 = (f32[512]{0:T(512)S(1)}, f32[512]{0:T(512)S(1)}) all-reduce(f32[512]{0:T(512)S(1)} %get-tuple-element.104, f32[512]{0:T(512)S(1)} %get-tuple-element.103), channel_id=1, replica_groups=mesh['batch'=4,'rows'=8] {'batch','rows'}, use_global_device_ids=true, to_apply=%region_7.8 | all-reduce | flops 1024 | bytes 8192 | tf_op jit(solution)/shard_map/psum | solution.py:63
  310.0 8.3 fusion.58
  318.3 41.4 %all-reduce.6 = (f32[2048]{0:T(1024)S(1)}, f32[2048]{0:T(1024)S(1)}) all-reduce(f32[2048]{0:T(1024)S(1)} %get-tuple-element.98, f32[2048]{0:T(1024)S(1)} %get-tuple-element.97), channel_id=1, replica_groups=mesh['batch'=4,'rows'=8] {'batch','rows'}, use_global_device_ids=true, to_apply=%region_11.12 | all-reduce | flops 4096 | bytes 32768 | tf_op jit(solution)/shard_map/psum | solution.py:63
  360.3 10.1 fusion.6
  370.5 3.4 all-to-all-start.1
  375.9 15.3 %all-gather = bf16[8,10,512]{2,1,0:T(8,128)(2,1)S(1)} all-gather(bf16[1,10,512]{2,1,0:T(8,128)(2,1)S(1)} %fusion.23), channel_id=1, replica_groups=mesh['batch'=4,'rows'=8] {'rows'}, dimensions={0}, use_global_device_ids=true | all-gather | bytes 92160 | tf_op jit(solution)/shard_map/all_gather | solution.py:203
  393.3 14.2 %all-gather.1 = bf16[8,10,512]{2,1,0:T(8,128)(2,1)S(1)} all-gather(bf16[1,10,512]{2,1,0:T(8,128)(2,1)S(1)} %fusion.24), channel_id=1, replica_groups=mesh['batch'=4,'rows'=8] {'rows'}, dimensions={0}, use_global_device_ids=true | all-gather | bytes 92160 | tf_op jit(solution)/shard_map/all_gather | solution.py:204
  411.7 2.4 fusion.3
  414.1 2.8 convert_reduce_fusion
  421.2 3.1 multiply_reduce_fusion.5
  425.0 2.8 fusion.71
  427.9 4.0 fusion.29
  432.4 16.0 %all_to_all.24 = bf16[8,10,1024]{2,1,0:T(8,128)(2,1)S(1)} all-to-all(bf16[8,10,1024]{2,1,0:T(8,128)(2,1)S(1)} %reshape.231), channel_id=1, replica_groups=mesh['batch'=4,'rows'=8] {'rows'}, dimensions={0} | all-to-all | bytes 327680 | tf_op jit(solution)/shard_map/all_to_all | solution.py:32
  448.4 2.7 convolution_bitcast_fusion.1
  451.2 2.7 convolution_bitcast_fusion
  454.5 3.0 fusion.4
  458.3 17.6 %all_to_all.25 = bf16[8,8,2048]{2,1,0:T(8,128)(2,1)S(1)} all-to-all(bf16[8,8,2048]{2,1,0:T(8,128)(2,1)S(1)} %bitcast_select_fusion), channel_id=1, replica_groups=mesh['batch'=4,'rows'=8] {'rows'}, dimensions={0} | all-to-all | bytes 524288 | tf_op jit(solution)/shard_map/all_to_all | solution.py:262
  476.4 14.8 %fusion.57 = (f32[2048]{0:T(1024)S(1)}, f32[2048]{0:T(1024)S(1)}, f32[1024,2048]{1,0:T(8,128)}) fusion(f32[2048]{0:T(1024)S(1)} %get-tuple-element.197, f32[1024,2048]{1,0:T(8,128)} %get-tuple-element.207, f32[2048]{0:T(1024)S(1)} %get-tuple-element.198, bf16[1024,2048]{1,0:T(8,128)(2,1)} %bitcast.154, f32[2048]{0:T(1024)} %param.41, ...), kind=kOutput, calls=%fused_computation.256 | convolution fusion | flops 309587968 | bytes 21297152 | tf_op jit(solution)/shard_map/dot_general | solution.py:46
  491.2 39.1 %all-reduce.5 = (f32[2048]{0:T(1024)S(1)}, f32[2048]{0:T(1024)S(1)}) all-reduce(f32[2048]{0:T(1024)S(1)} %get-tuple-element.96, f32[2048]{0:T(1024)S(1)} %get-tuple-element.95), channel_id=1, replica_groups=mesh['batch'=4,'rows'=8] {'batch','rows'}, use_global_device_ids=true, to_apply=%region_22.23 | all-reduce | flops 4096 | bytes 32768 | tf_op jit(solution)/shard_map/psum | solution.py:265
  530.3 7.4 multiply_convert_fusion
  539.8 4.9 fusion.53
  544.8 7.8 fusion.60
  552.5 42.7 %all-reduce.4 = (f32[512]{0:T(512)S(1)}, f32[512]{0:T(512)S(1)}) all-reduce(f32[512]{0:T(512)S(1)} %get-tuple-element.102, f32[512]{0:T(512)S(1)} %get-tuple-element.101), channel_id=1, replica_groups=mesh['batch'=4,'rows'=8] {'batch','rows'}, use_global_device_ids=true, to_apply=%region_26.27 | all-reduce | flops 1024 | bytes 8192 | tf_op jit(solution)/shard_map/psum | solution.py:70
  595.2 2.9 multiply_convert_fusion.7
  599.4 2.7 collective-permute-start.5
  603.6 6.7 copy.127
  610.3 3.8 select_maximum_fusion
  614.1 3.5 fusion.64
  617.6 2.3 copy.119
  619.9 2.4 copy.120
  626.9 2.3 copy.123
  642.3 7.2 fusion.59
  649.5 51.3 %all-reduce.3 = (f32[512]{0:T(512)S(1)}, f32[512]{0:T(512)S(1)}, f32[512]{0:T(512)}, f32[512]{0:T(512)}, f32[80]{0:T(128)}) all-reduce(f32[512]{0:T(512)S(1)} %get-tuple-element.100, f32[512]{0:T(512)S(1)} %get-tuple-element.99, f32[512]{0:T(512)S(1)} %copy-done.36, ...), channel_id=1, replica_groups=mesh['batch'=4,'rows'=8] {'batch','rows'}, use_global_device_ids=true, to_apply=%region_30.31 | all-reduce | flops 2128 | bytes 17024 | tf_op jit(solution)/shard_map/psum | solution.py:70
  700.8 7.6 convolution_bitcast_fusion.2
  708.5 11.4 %fusion.70 = f32[4608,512]{1,0:T(8,128)} fusion(bf16[1024,4608]{0,1:T(8,128)(2,1)} %constant_dynamic-update-slice_fusion.8, bf16[1024,512]{0,1:T(8,128)(2,1)S(1)} %multiply_convert_fusion.7), kind=kOutput, calls=%fused_computation.268 | convolution fusion | flops 4831838208 | bytes 19922944 | tf_op jit(solution)/shard_map/dot_general | solution.py:46
  731.1 36.1 %reduce-scatter.20.cloned.1.call-done = f32[256,512]{0,1:T(8,128)} async-done(((f32[2048,512]{0,1:T(8,128)}), f32[256,512]{0,1:T(8,128)}) %reduce-scatter.20.cloned.1.call-update) | async-done | bytes 524304 | tf_op jit(solution)/shard_map/reduce_scatter | solution.py:300
  769.1 98.0 %reduce-scatter.24.cloned.1.call-done = f32[576,512]{1,0:T(8,128)} async-done(((f32[4608,512]{1,0:T(8,128)}), f32[576,512]{1,0:T(8,128)}) %reduce-scatter.24.cloned.1.call-update) | async-done | bytes 1179664 | tf_op jit(solution)/shard_map/reduce_scatter | solution.py:301
  870.9 9.7 add_convert_fusion
  880.6 29.3 %all-reduce.11.cloned.1.call-done = bf16[512,80]{0,1:T(8,128)(2,1)} async-done(((bf16[512,80]{0,1:T(8,128)(2,1)}), bf16[512,80]{0,1:T(8,128)(2,1)}) %all-reduce.11.cloned.1.call-update) | async-done | bytes 81936
  911.3 26.3 %reduce-scatter.48.cloned.1.call-done = bf16[128,256]{1,0:T(8,128)(2,1)} async-done(((bf16[512,256]{1,0:T(8,128)(2,1)}), bf16[128,256]{1,0:T(8,128)(2,1)}) %reduce-scatter.48.cloned.1.call-update) | async-done | bytes 65552
  939.2 25.1 %reduce-scatter.42.cloned.1.call-done = bf16[64,512]{1,0:T(8,128)(2,1)} async-done(((bf16[64,2048]{1,0:T(8,128)(2,1)}), bf16[64,512]{1,0:T(8,128)(2,1)}) %reduce-scatter.42.cloned.1.call-update) | async-done | bytes 65552 | tf_op jit(solution)/shard_map/reduce_scatter | solution.py:328
  965.8 25.5 %reduce-scatter.34.cloned.1.call-done = bf16[256,128]{0,1:T(8,128)(2,1)} async-done(((bf16[256,512]{0,1:T(8,128)(2,1)}), bf16[256,128]{0,1:T(8,128)(2,1)}) %reduce-scatter.34.cloned.1.call-update) | async-done | bytes 65552 | tf_op jit(solution)/shard_map/reduce_scatter | solution.py:322
  992.9 25.3 %reduce-scatter.38.cloned.1.call-done = bf16[256,128]{0,1:T(8,128)(2,1)} async-done(((bf16[256,512]{0,1:T(8,128)(2,1)}), bf16[256,128]{0,1:T(8,128)(2,1)}) %reduce-scatter.38.cloned.1.call-update) | async-done | bytes 65552 | tf_op jit(solution)/shard_map/reduce_scatter | solution.py:325
  1019.8 25.4 %reduce-scatter.28.cloned.1.call-done = bf16[64,512]{1,0:T(8,128)(2,1)} async-done(((bf16[64,2048]{1,0:T(8,128)(2,1)}), bf16[64,512]{1,0:T(8,128)(2,1)}) %reduce-scatter.28.cloned.1.call-update) | async-done | bytes 65552 | tf_op jit(solution)/shard_map/reduce_scatter | solution.py:316
  1046.6 25.9 %reduce-scatter.22.cloned.1.call-done = bf16[256,128]{0,1:T(8,128)(2,1)} async-done(((bf16[256,512]{0,1:T(8,128)(2,1)}), bf16[256,128]{0,1:T(8,128)(2,1)}) %reduce-scatter.22.cloned.1.call-update) | async-done | bytes 65552 | tf_op jit(solution)/shard_map/reduce_scatter | solution.py:310
  1074.2 27.0 %reduce-scatter.46.cloned.1.call-done = bf16[128,576]{1,0:T(8,128)(2,1)} async-done(((bf16[512,576]{1,0:T(8,128)(2,1)}), bf16[128,576]{1,0:T(8,128)(2,1)}) %reduce-scatter.46.cloned.1.call-update) | async-done | bytes 147472
  (481 shorter events, 104.3 us)
Async XLA Ops:
  7.2 366.8 %copy-start = (bf16[10,2048]{1,0:T(8,128)(2,1)S(1)}, bf16[10,2048]{1,0:T(8,128)(2,1)}, u32[]{:S(2)}) copy-start(bf16[10,2048]{1,0:T(8,128)(2,1)} %param.45) | copy-start | bytes 122884
  7.2 250.5 %all-gather.9.cloned.1.call-start = ((), (), s32[]{:S(2)}) async-start(), calls=%async_computation.19 | async-start | bytes 5308416 | tf_op jit(solution)/shard_map/all_gather | solution.py:134
  8.0 301.8 %all-gather.11.cloned.1.call-start = ((), (), s32[]{:S(2)}) async-start(), calls=%async_computation.20 | async-start | bytes 2359296 | tf_op jit(solution)/shard_map/all_gather | solution.py:135
  8.7 365.2 %all-gather.15.cloned.1.call-start = ((), (), s32[]{:S(2)}) async-start(), calls=%async_computation.22 | async-start | bytes 2359296 | tf_op jit(solution)/shard_map/all_gather | solution.py:137
  9.5 381.9 %all-gather.17.cloned.1.call-start = ((), (), s32[]{:S(2)}) async-start(), calls=%async_computation.23 | async-start | bytes 2359296 | tf_op jit(solution)/shard_map/all_gather | solution.py:138
  10.0 398.8 %all-gather.13.cloned.1.call-start = ((), (), s32[]{:S(2)}) async-start(), calls=%async_computation.21 | async-start | bytes 2359296 | tf_op jit(solution)/shard_map/all_gather | solution.py:136
  10.6 8.7 collective-permute-start
  20.4 36.5 %collective-permute-start.1 = (bf16[512,512]{1,0:T(8,128)(2,1)S(1)}, bf16[512,512]{1,0:T(8,128)(2,1)S(1)}, u32[]{:S(2)}, u32[]{:S(2)}) collective-permute-start(bf16[512,512]{1,0:T(8,128)(2,1)S(1)} %pad_maximum_fusion.4), channel_id=1, source_target_pairs={{0,6},{1,7},{2,0},{3,1},{4,2},{5,3},{6,4},{7,5},{8,14},{9,15},{10,... | collective-permute-start | bytes 1572872 | tf_op jit(solution)/shard_map/ppermute | solution.py:121
  57.9 58.3 %collective-permute-start.2 = (bf16[1024,512]{1,0:T(8,128)(2,1)S(1)}, bf16[1024,512]{1,0:T(8,128)(2,1)S(1)}, u32[]{:S(2)}, u32[]{:S(2)}) collective-permute-start(bf16[1024,512]{1,0:T(8,128)(2,1)S(1)} %pad_maximum_fusion), channel_id=1, source_target_pairs={{0,4},{1,5},{2,6},{3,7},{4,0},{5,1},{6,2},{7,3},{8,12},{9,13},{10,... | collective-permute-start | bytes 3145736 | tf_op jit(solution)/shard_map/ppermute | solution.py:121
  57.9 156.6 %all-to-all-start = ((s32[8,1,8]{2,1,0:T(1,128)}), s32[8,1,8]{2,1,0:T(1,128)S(1)}, u32[]{:S(2)}, u32[]{:S(2)}) async-start(s32[8,1,8]{2,1,0:T(1,128)} %bitcast.1), calls=%async_computation | async-start | bytes 8192 | tf_op jit(solution)/shard_map/all_to_all | solution.py:191
  62.1 349.5 %all-gather.19.cloned.1.call-start = ((), (), s32[]{:S(2)}) async-start(), calls=%async_computation.24 | async-start | bytes 2359296 | tf_op jit(solution)/shard_map/all_gather | solution.py:139
  164.3 51.6 %collective-permute-start.3 = (bf16[64,1,16,512]{3,2,0,1:T(8,128)(2,1)}, bf16[64,1,16,512]{3,2,0,1:T(8,128)(2,1)}, u32[]{:S(2)}, u32[]{:S(2)}) collective-permute-start(bf16[64,1,16,512]{3,2,0,1:T(8,128)(2,1)} %bitcast.4), channel_id=1, source_target_pairs={{0,1},{1,2},{2,3},{3,4},{4,5},{5,6},{6,7},{8,9},{9,10},{10,11},{11... | collective-permute-start | bytes 3145736 | tf_op jit(solution)/shard_map/ppermute | solution.py:15
  167.0 48.8 %collective-permute-start.4 = (bf16[64,1,16,512]{3,2,0,1:T(8,128)(2,1)}, bf16[64,1,16,512]{3,2,0,1:T(8,128)(2,1)S(1)}, u32[]{:S(2)}, u32[]{:S(2)}) collective-permute-start(bf16[64,1,16,512]{3,2,0,1:T(8,128)(2,1)} %bitcast.4), channel_id=1, source_target_pairs={{1,0},{2,1},{3,2},{4,3},{5,4},{6,5},{7,6},{9,8},{10,9},{11,10},{12... | collective-permute-start | bytes 3145736 | tf_op jit(solution)/shard_map/ppermute | solution.py:17
  168.9 190.8 %copy-start.44 = (s32[64]{0:T(128)}, s32[64]{0:T(128)S(1)}, u32[]{:S(2)}) copy-start(s32[64]{0:T(128)S(1)} %get-tuple-element.149) | copy-start | bytes 772
  168.9 190.8 %copy-start.46 = (s32[64]{0:T(128)}, s32[64]{0:T(128)S(1)}, u32[]{:S(2)}) copy-start(s32[64]{0:T(128)S(1)} %get-tuple-element.150) | copy-start | bytes 772
  168.9 190.8 %copy-start.48 = (s32[64]{0:T(128)}, s32[64]{0:T(128)S(1)}, u32[]{:S(2)}) copy-start(s32[64]{0:T(128)S(1)} %get-tuple-element.151) | copy-start | bytes 772
  168.9 190.8 %copy-start.50 = (s32[64]{0:T(128)}, s32[64]{0:T(128)S(1)}, u32[]{:S(2)}) copy-start(s32[64]{0:T(128)S(1)} %get-tuple-element.152) | copy-start | bytes 772
  169.0 190.8 %copy-start.52 = (s32[64]{0:T(128)}, s32[64]{0:T(128)S(1)}, u32[]{:S(2)}) copy-start(s32[64]{0:T(128)S(1)} %get-tuple-element.153) | copy-start | bytes 772
  169.0 190.8 %copy-start.54 = (s32[64]{0:T(128)}, s32[64]{0:T(128)S(1)}, u32[]{:S(2)}) copy-start(s32[64]{0:T(128)S(1)} %get-tuple-element.154) | copy-start | bytes 772
  169.0 190.8 %copy-start.56 = (s32[64]{0:T(128)}, s32[64]{0:T(128)S(1)}, u32[]{:S(2)}) copy-start(s32[64]{0:T(128)S(1)} %get-tuple-element.155) | copy-start | bytes 772
  169.0 190.8 %copy-start.58 = (s32[64]{0:T(128)}, s32[64]{0:T(128)S(1)}, u32[]{:S(2)}) copy-start(s32[64]{0:T(128)S(1)} %get-tuple-element.156) | copy-start | bytes 772
  169.0 190.8 %copy-start.60 = (s32[64]{0:T(128)}, s32[64]{0:T(128)S(1)}, u32[]{:S(2)}) copy-start(s32[64]{0:T(128)S(1)} %get-tuple-element.157) | copy-start | bytes 772
  170.2 189.7 %copy-start.82 = (s32[64]{0:T(128)}, s32[64]{0:T(128)S(1)}, u32[]{:S(2)}) copy-start(s32[64]{0:T(128)S(1)} %get-tuple-element.111) | copy-start | bytes 772
  170.2 189.7 %copy-start.84 = (s32[64]{0:T(128)}, s32[64]{0:T(128)S(1)}, u32[]{:S(2)}) copy-start(s32[64]{0:T(128)S(1)} %get-tuple-element.112) | copy-start | bytes 772
  170.2 189.7 %copy-start.86 = (s32[64]{0:T(128)}, s32[64]{0:T(128)S(1)}, u32[]{:S(2)}) copy-start(s32[64]{0:T(128)S(1)} %get-tuple-element.113) | copy-start | bytes 772
  170.2 189.7 %copy-start.88 = (s32[64]{0:T(128)}, s32[64]{0:T(128)S(1)}, u32[]{:S(2)}) copy-start(s32[64]{0:T(128)S(1)} %get-tuple-element.114) | copy-start | bytes 772
  170.2 189.7 %copy-start.90 = (s32[64]{0:T(128)}, s32[64]{0:T(128)S(1)}, u32[]{:S(2)}) copy-start(s32[64]{0:T(128)S(1)} %get-tuple-element.115) | copy-start | bytes 772
  170.2 189.7 %copy-start.92 = (s32[64]{0:T(128)}, s32[64]{0:T(128)S(1)}, u32[]{:S(2)}) copy-start(s32[64]{0:T(128)S(1)} %get-tuple-element.116) | copy-start | bytes 772
  170.2 189.7 %copy-start.94 = (s32[64]{0:T(128)}, s32[64]{0:T(128)S(1)}, u32[]{:S(2)}) copy-start(s32[64]{0:T(128)S(1)} %get-tuple-element.117) | copy-start | bytes 772
  170.2 189.7 %copy-start.96 = (s32[64]{0:T(128)}, s32[64]{0:T(128)S(1)}, u32[]{:S(2)}) copy-start(s32[64]{0:T(128)S(1)} %get-tuple-element.118) | copy-start | bytes 772
  170.2 189.7 %copy-start.98 = (s32[64]{0:T(128)}, s32[64]{0:T(128)S(1)}, u32[]{:S(2)}) copy-start(s32[64]{0:T(128)S(1)} %get-tuple-element.119) | copy-start | bytes 772
  170.2 189.7 %copy-start.100 = (s32[64]{0:T(128)}, s32[64]{0:T(128)S(1)}, u32[]{:S(2)}) copy-start(s32[64]{0:T(128)S(1)} %get-tuple-element.120) | copy-start | bytes 772
  170.2 189.7 %copy-start.102 = (s32[64]{0:T(128)}, s32[64]{0:T(128)S(1)}, u32[]{:S(2)}) copy-start(s32[64]{0:T(128)S(1)} %get-tuple-element.121) | copy-start | bytes 772
  170.2 189.7 %copy-start.104 = (s32[64]{0:T(128)}, s32[64]{0:T(128)S(1)}, u32[]{:S(2)}) copy-start(s32[64]{0:T(128)S(1)} %get-tuple-element.122) | copy-start | bytes 772
  171.5 188.5 %copy-start.120 = (f32[64]{0:T(128)}, f32[64]{0:T(128)S(1)}, u32[]{:S(2)}) copy-start(f32[64]{0:T(128)S(1)} %get-tuple-element.130) | copy-start | bytes 772
  171.5 188.5 %copy-start.122 = (f32[64]{0:T(128)}, f32[64]{0:T(128)S(1)}, u32[]{:S(2)}) copy-start(f32[64]{0:T(128)S(1)} %get-tuple-element.131) | copy-start | bytes 772
  171.5 188.5 %copy-start.124 = (f32[64]{0:T(128)}, f32[64]{0:T(128)S(1)}, u32[]{:S(2)}) copy-start(f32[64]{0:T(128)S(1)} %get-tuple-element.132) | copy-start | bytes 772
  171.5 188.5 %copy-start.125 = (f32[64]{0:T(128)}, f32[64]{0:T(128)S(1)}, u32[]{:S(2)}) copy-start(f32[64]{0:T(128)S(1)} %get-tuple-element.133) | copy-start | bytes 772
  171.5 188.5 %copy-start.126 = (f32[64]{0:T(128)}, f32[64]{0:T(128)S(1)}, u32[]{:S(2)}) copy-start(f32[64]{0:T(128)S(1)} %get-tuple-element.134) | copy-start | bytes 772
  214.5 145.6 %copy-start.62 = (f32[64]{0:T(128)}, f32[64]{0:T(128)S(1)}, u32[]{:S(2)}) copy-start(f32[64]{0:T(128)S(1)} %get-tuple-element.158) | copy-start | bytes 772
  214.5 145.6 %copy-start.64 = (f32[64]{0:T(128)}, f32[64]{0:T(128)S(1)}, u32[]{:S(2)}) copy-start(f32[64]{0:T(128)S(1)} %get-tuple-element.159) | copy-start | bytes 772
  214.5 145.6 %copy-start.66 = (f32[64]{0:T(128)}, f32[64]{0:T(128)S(1)}, u32[]{:S(2)}) copy-start(f32[64]{0:T(128)S(1)} %get-tuple-element.160) | copy-start | bytes 772
  214.5 145.6 %copy-start.68 = (f32[64]{0:T(128)}, f32[64]{0:T(128)S(1)}, u32[]{:S(2)}) copy-start(f32[64]{0:T(128)S(1)} %get-tuple-element.161) | copy-start | bytes 772
  370.5 37.1 %all-to-all-start.1 = ((bf16[8,8,2048]{2,1,0:T(8,128)(2,1)}), bf16[8,8,2048]{2,1,0:T(8,128)(2,1)S(1)}, u32[]{:S(2)}, u32[]{:S(2)}) async-start(bf16[8,8,2048]{2,1,0:T(8,128)(2,1)} %fusion.6), calls=%async_computation.1 | async-start | bytes 524288 | tf_op jit(solution)/shard_map/all_to_all | solution.py:190
  373.9 346.0 %reduce-scatter.44.cloned.1.call-start = ((), (), s32[]{:S(2)}) async-start(), calls=%async_computation.37 | async-start | bytes 1474560 | tf_op jit(solution)/shard_map/reduce_scatter | solution.py:307
  418.3 303.3 %reduce-scatter.30.cloned.1.call-start = ((), (), s32[]{:S(2)}) async-start(), calls=%async_computation.30 | async-start | bytes 4718592 | tf_op jit(solution)/shard_map/reduce_scatter | solution.py:303
  427.8 295.8 %reduce-scatter.40.cloned.1.call-start = ((), (), s32[]{:S(2)}) async-start(), calls=%async_computation.35 | async-start | bytes 4718592 | tf_op jit(solution)/shard_map/reduce_scatter | solution.py:306
  431.9 293.6 %reduce-scatter.32.cloned.1.call-start = ((), (), s32[]{:S(2)}) async-start(), calls=%async_computation.31 | async-start | bytes 4718592 | tf_op jit(solution)/shard_map/reduce_scatter | solution.py:304
  451.2 276.2 %reduce-scatter.36.cloned.1.call-start = ((), (), s32[]{:S(2)}) async-start(), calls=%async_computation.33 | async-start | bytes 4718592 | tf_op jit(solution)/shard_map/reduce_scatter | solution.py:305
  454.3 274.9 %reduce-scatter.26.cloned.1.call-start = ((), (), s32[]{:S(2)}) async-start(), calls=%async_computation.28 | async-start | bytes 4718592 | tf_op jit(solution)/shard_map/reduce_scatter | solution.py:302
  544.7 222.5 %reduce-scatter.20.cloned.1.call-start = ((), (), s32[]{:S(2)}) async-start(), calls=%async_computation.25 | async-start | bytes 4718592 | tf_op jit(solution)/shard_map/reduce_scatter | solution.py:300
  599.4 10.8 collective-permute-start.5
  602.1 8.1 collective-permute-start.6
  700.8 170.1 %copy-start.42 = (f32[512]{0:T(512)}, f32[512]{0:T(512)S(1)}, u32[]{:S(2)}) copy-start(f32[512]{0:T(512)S(1)} %get-tuple-element.167) | copy-start | bytes 6148
  708.4 158.7 %reduce-scatter.24.cloned.1.call-start = ((), (), s32[]{:S(2)}) async-start(), calls=%async_computation.27 | async-start | bytes 10616832 | tf_op jit(solution)/shard_map/reduce_scatter | solution.py:301
  719.8 190.1 %all-reduce.11.cloned.1.call-start = ((), (), s32[]{:S(2)}) async-start(), calls=%async_computation.40 | async-start | bytes 163840
  721.5 216.1 %reduce-scatter.48.cloned.1.call-start = ((), (), s32[]{:S(2)}) async-start(), calls=%async_computation.39 | async-start | bytes 327680
  723.5 240.8 %reduce-scatter.42.cloned.1.call-start = ((), (), s32[]{:S(2)}) async-start(), calls=%async_computation.36 | async-start | bytes 327680 | tf_op jit(solution)/shard_map/reduce_scatter | solution.py:328
  725.4 265.9 %reduce-scatter.34.cloned.1.call-start = ((), (), s32[]{:S(2)}) async-start(), calls=%async_computation.32 | async-start | bytes 327680 | tf_op jit(solution)/shard_map/reduce_scatter | solution.py:322
  727.3 290.9 %reduce-scatter.38.cloned.1.call-start = ((), (), s32[]{:S(2)}) async-start(), calls=%async_computation.34 | async-start | bytes 327680 | tf_op jit(solution)/shard_map/reduce_scatter | solution.py:325
  729.2 315.9 %reduce-scatter.28.cloned.1.call-start = ((), (), s32[]{:S(2)}) async-start(), calls=%async_computation.29 | async-start | bytes 327680 | tf_op jit(solution)/shard_map/reduce_scatter | solution.py:316
  731.1 341.5 %reduce-scatter.22.cloned.1.call-start = ((), (), s32[]{:S(2)}) async-start(), calls=%async_computation.26 | async-start | bytes 327680 | tf_op jit(solution)/shard_map/reduce_scatter | solution.py:310
  769.0 332.1 %reduce-scatter.46.cloned.1.call-start = ((), (), s32[]{:S(2)}) async-start(), calls=%async_computation.38 | async-start | bytes 819200
  870.9 232.1 %copy-start.1 = (bf16[10,2048]{1,0:T(8,128)(2,1)S(1)}, bf16[10,2048]{1,0:T(8,128)(2,1)}, u32[]{:S(2)}) copy-start(bf16[10,2048]{1,0:T(8,128)(2,1)} %param.45) | copy-start | bytes 122884
  (118 other events, 3983.8 us)
Sparse Core Ops, SparseCore 0:
  9.7 92.7 all-gather.8
  104.1 31.4 all-gather.10
  137.2 29.0 all-gather.14
  167.8 35.2 all-gather.16
  204.6 30.8 all-gather.12
  236.9 28.5 all-gather.18
  418.4 34.9 reduce-scatter.43
  455.7 53.5 reduce-scatter.29
  511.5 49.1 reduce-scatter.39
  562.8 50.1 reduce-scatter.31
  615.4 49.3 reduce-scatter.35
  667.0 49.1 reduce-scatter.25
  719.1 48.1 reduce-scatter.19
  769.4 97.6 reduce-scatter.23
  870.4 39.4 all-reduce.10
  912.7 24.8 reduce-scatter.47
  940.2 24.0 reduce-scatter.41
  967.2 24.0 reduce-scatter.33
  994.1 24.0 reduce-scatter.37
  1021.0 24.0 reduce-scatter.27
  1048.5 24.0 reduce-scatter.21
  1075.7 25.3 reduce-scatter.45
